TPU v7x, 32 devices: a whole 2x2x4 slice. The times are simulated.
32 devices in a mesh: grp: 4 (over x, core), col: 8 (over z, y).
Axes of the slice: x: 2, y: 2, z: 4, core: 2. Of those that a mesh axis runs over, the one named last changes fastest.
Arguments:
- diag_blocks: float32 [4096, 1024], P('grp', 'col'), may hold values from -8 to 48, as said below
- coupling: float32 [24576, 1024], P(('grp', 'col')), may hold values from -4 to 4
- parent_front: float32 [12288, 12288], P('grp', 'col'), may hold values from -6 to 6
- index_maps: int32 [4, 48], replicated, may hold values from 0 to 95, as said below
Outputs:
- assembled: float32 [12288, 12288], P('grp', 'col')
- diag_factor: float32 [4096, 1024], P('grp', 'col')
- panel: float32 [24576, 1024], P(('grp', 'col'))
Inputs may be any that keep to these rules, and one draw needn't show every extreme that they name: `diag_blocks`: each front's block of 1024 rows is symmetric positive definite. `index_maps`: the 48 entries of one row are distinct, and every parent block is named by some front.
All inputs are finite; a program needn't handle non-finite values.
Results may differ from a plain program's by a relative error of at most 0.0027.
Values may be sent and summed in bfloat16 or wider, within the bound.
No kernel may reach another device: no remote copies, remote signals or barrier semaphores. Data moves between devices by JAX's collectives and lax.ppermute only.
A program may use at most 192 MiB of HBM per device.

v0:
```python
import jax
import jax.numpy as jnp
from jax import lax
from jax.sharding import PartitionSpec as P

FRONTS = 4
BLK = 128
SBLK = 48
PBLK = 96


def swapped(block, axis, stride):
    count = lax.axis_size(axis)
    route = []
    for low in range(count):
        high = low | 1 << stride
        if high != low and high < count:
            route += [(low, high), (high, low)]
    return lax.ppermute(block, axis, route)


def place_rows(slab_blocks, source_block, present_count, count):
    picked = slab_blocks[jnp.arange(FRONTS)[:, None], source_block]
    picked = jnp.where(present_count[:, :, None, None] > 0, picked, jnp.zeros_like(picked))
    return jnp.transpose(picked, (1, 2, 0, 3)).reshape(count * BLK, -1)


def on_device(diag_blocks, coupling, parent_front, index_maps):
    groups = lax.axis_size("grp") // FRONTS
    swap_depth = groups.bit_length() - 1
    grp_index = lax.axis_index("grp")
    col_index = lax.axis_index("col")
    gathered = lax.all_gather(diag_blocks, "col", axis=1, tiled=True)
    for bit_pos in range(swap_depth):
        partner = swapped(gathered, "grp", bit_pos)
        is_upper = grp_index // 2**bit_pos % 2 == 1
        lower_half = jnp.where(is_upper, partner, gathered)
        upper_half = jnp.where(is_upper, gathered, partner)
        gathered = jnp.concatenate([lower_half, upper_half], axis=0)
    factor = jnp.linalg.cholesky(gathered)
    rows_here = diag_blocks.shape[0]
    col_width = diag_blocks.shape[1]
    local_start = grp_index % groups * rows_here
    factor_tile = lax.dynamic_slice(
        factor, (local_start, col_index * col_width), (rows_here, col_width)
    )
    panel_rows = lax.linalg.triangular_solve(
        factor, coupling, left_side=False, lower=True, transpose_a=True
    )
    panel_half = panel_rows.astype(jnp.bfloat16)
    panel_tiles = lax.all_to_all(panel_half, "col", split_axis=1, concat_axis=0, tiled=True)
    panel_slab = lax.all_gather(panel_tiles, "grp", axis=0, tiled=True)
    slab_blocks = panel_slab.reshape(FRONTS, SBLK, BLK, -1)
    parent_ids = jnp.arange(PBLK, dtype=jnp.int32)
    matches = (index_maps[:, :, None] == parent_ids[None, None, :]).astype(jnp.int32)
    present_count = jnp.sum(matches, axis=1)
    source_block = jnp.sum(matches * jnp.arange(SBLK, dtype=jnp.int32)[None, :, None], axis=1)
    row_count = parent_front.shape[0]
    contract = (((1,), (1,)), ((), ()))
    every_part = place_rows(slab_blocks, source_block, present_count, PBLK)
    col_operand = lax.all_to_all(every_part, "col", split_axis=0, concat_axis=1, tiled=True)
    row_part = lax.dynamic_slice_in_dim(every_part, grp_index * row_count, row_count, 0)
    update = lax.dot_general(
        lax.all_gather(row_part, "col", axis=1, tiled=True),
        col_operand,
        contract,
        preferred_element_type=jnp.float32,
    )
    merged = parent_front - update
    return (merged, factor_tile, panel_rows)


def solution(mesh):
    in_specs = (P("grp", "col"), P(("grp", "col"), None), P("grp", "col"), P())
    out_specs = (P("grp", "col"), P("grp", "col"), P(("grp", "col"), None))
    return jax.shard_map(
        on_device, mesh=mesh, in_specs=in_specs, out_specs=out_specs, check_vma=False
    )
```

profile of v0, /device:TPU:29, one launch (start us, length us, event | category | flops | bytes accessed | tf_op | source)
XLA Modules:
  0.0 1300.4 jit_solution(12328912837952660922)
XLA Ops:
  9.3 72.7 %all-gather.4.cloned.1.call-done = f32[1024,1024]{0,1:T(8,128)} async-done(((f32[1024,128]{0,1:T(8,128)}), f32[1024,1024]{0,1:T(8,128)}) %all-gather.4.cloned.1.call-update) | async-done | bytes 4194320 | tf_op jit(solution)/shard_map/all_gather | solution.py:33
  93.7 11.7 cholesky.223
  105.5 9.8 custom-call.62
  121.7 12.2 cholesky.244
  147.6 11.7 cholesky.468
  160.7 9.8 custom-call.64
  174.0 11.8 cholesky.487
  200.4 11.7 cholesky.506
  213.4 10.0 custom-call.66
  226.7 11.7 cholesky.526
  252.5 12.1 cholesky.546
  278.5 11.7 cholesky.564
  304.1 29.0 %while.1 = (s32[]{:T(128)}, f32[1024,1024]{1,0:T(8,128)}, s32[8,2]{0,1:T(2,128)S(1)}, f32[8,128,128]{2,1,0:T(8,128)}, s32[]{:T(128)}) while((s32[]{:T(128)}, f32[1024,1024]{1,0:T(8,128)}, s32[8,2]{0,1:T(2,128)S(1)}, f32[8,128,128]{2,1,0:T(8,128)}, s32[]{:T(128)}) %tuple.72), condition=%wide.while_cond, body=%wide.while_body.sunk | while | flops 2 | bytes 132205 | solution.py:47
  333.2 80.2 %custom-call.69 = f32[8,128,128]{1,2,0:T(8,128)} custom-call(f32[8,128,128]{2,1,0:T(8,128)} %get-tuple-element.10), custom_call_target="InvertDiagBlocksLowerTriangular" | custom-call | tf_op jit(solution)/shard_map/triangular_solve | solution.py:47
  445.4 40.0 %all_to_all.35 = bf16[768,8,128]{0,2,1:T(8,128)(2,1)S(1)} all-to-all(bf16[768,8,128]{0,2,1:T(8,128)(2,1)S(1)} %get-tuple-element.103), channel_id=1, replica_groups=mesh['grp'=4,'col'=8] {'col'}, dimensions={1} | all-to-all | bytes 3145728 | tf_op jit(solution)/shard_map/all_to_all | solution.py:51
  487.3 47.8 %all-gather.6.cloned.1.call-done = bf16[24576,128]{1,0:T(8,128)(2,1)} async-done(((bf16[6144,128]{1,0:T(8,128)(2,1)}), bf16[24576,128]{1,0:T(8,128)(2,1)}) %all-gather.6.cloned.1.call-update) | async-done | bytes 6291472 | tf_op jit(solution)/shard_map/all_gather | solution.py:52
  535.1 19.7 %gather_fusion = bf16[384,128,128]{2,1,0:T(8,128)(2,1)} fusion(bf16[4,48,128,128]{3,2,1,0:T(8,128)(2,1)} %bitcast.155, s32[384]{0:T(512)S(1)} %reshape.147), kind=kCustom, calls=%fused_computation | custom fusion | bytes 25168896 | tf_op jit(solution)/shard_map/gather | solution.py:23
  554.8 10.6 broadcast_select_fusion
  565.4 16.5 %copy.32 = bf16[96,128,4,128]{1,0,3,2:T(8,128)(2,1)} copy(bf16[96,128,4,128]{3,1,0,2:T(8,128)(2,1)} %broadcast_select_fusion) | data formatting | bytes 25165824 | tf_op jit(solution)/shard_map/jit(_where)/select_n | solution.py:24
  593.4 23.6 %all_to_all.29 = bf16[8,1536,512]{1,0,2:T(8,128)(2,1)} reshape(bf16[96,128,4,128]{1,0,3,2:T(8,128)(2,1)} %copy.32) | data formatting | bytes 25165824 | tf_op jit(solution)/shard_map/all_to_all | solution.py:61
  617.0 12.9 copy.34
  640.3 377.6 %all-to-all-done.1 = bf16[8,1536,512]{1,2,0:T(8,128)(2,1)} async-done(((bf16[8,1536,512]{1,2,0:T(8,128)(2,1)}), bf16[8,1536,512]{1,2,0:T(8,128)(2,1)}, u32[]{:S(2)}, u32[]{:S(2)}) %all-to-all-start.1) | async-done | bytes 12582944 | tf_op jit(solution)/shard_map/all_to_all | solution.py:61
  1017.9 226.9 %all-gather.8.cloned.1.call-done = bf16[3072,4096]{0,1:T(8,128)(2,1)} async-done(((bf16[3072,512]{0,1:T(8,128)(2,1)}), bf16[3072,4096]{0,1:T(8,128)(2,1)}) %all-gather.8.cloned.1.call-update) | async-done | bytes 25165840 | tf_op jit(solution)/shard_map/all_gather | solution.py:64
  1244.8 48.9 %convolution_subtract_fusion = f32[3072,1536]{1,0:T(8,128)} fusion(f32[3072,1536]{1,0:T(8,128)} %param.6, bf16[3072,4096]{0,1:T(8,128)(2,1)} %all-gather.8.cloned.1.call-done, bf16[1536,4096]{0,1:T(8,128)(2,1)} %bitcast.40), kind=kOutput, calls=%fused_computation.3 | convolution fusion | flops 38659424256 | bytes 75497472 | tf_op jit(solution)/shard_map/dot_general | solution.py:63
  (123 shorter events, 179.2 us)
Async XLA Ops:
  7.2 74.9 %all-gather.4.cloned.1.call-start = ((), (), s32[]{:S(2)}) async-start(), calls=%async_computation.2 | async-start | bytes 4718592 | tf_op jit(solution)/shard_map/all_gather | solution.py:33
  9.3 525.9 %all-gather.6.cloned.1.call-start = ((), (), s32[]{:S(2)}) async-start(), calls=%async_computation.3 | async-start | bytes 7864320 | tf_op jit(solution)/shard_map/all_gather | solution.py:52
  91.8 1.9 copy-start
  297.2 116.2 %copy-start.3 = (f32[768,1024]{1,0:T(8,128)S(1)}, f32[768,1024]{1,0:T(8,128)}, u32[]{:S(2)}) copy-start(f32[768,1024]{1,0:T(8,128)} %param.5) | copy-start | bytes 9437188
  413.4 3.2 copy-start.4
  438.9 46.5 %copy-start.1 = (f32[768,1024]{0,1:T(8,128)}, f32[768,1024]{0,1:T(8,128)S(1)}, u32[]{:S(2)}) copy-start(f32[768,1024]{0,1:T(8,128)S(1)} %get-tuple-element.40) | copy-start | bytes 9437188
  485.4 1.6 copy-start.5
  487.0 757.7 %all-gather.8.cloned.1.call-start = ((), (), s32[]{:S(2)}) async-start(), calls=%async_computation.4 | async-start | bytes 28311552 | tf_op jit(solution)/shard_map/all_gather | solution.py:64
  629.9 6.0 copy-start.2
  629.9 387.9 %all-to-all-start.1 = ((bf16[8,1536,512]{1,2,0:T(8,128)(2,1)}), bf16[8,1536,512]{1,2,0:T(8,128)(2,1)}, u32[]{:S(2)}, u32[]{:S(2)}) async-start(bf16[8,1536,512]{1,2,0:T(8,128)(2,1)} %copy.34), calls=%async_computation.1 | async-start | bytes 25165824 | tf_op jit(solution)/shard_map/all_to_all | solution.py:61
Sparse Core Ops, SparseCore 0:
  10.7 71.3 all-gather.3
  487.1 47.9 all-gather.5
  593.5 651.2 all-gather.7
where the time goes:
time: 1310 us; the launch traced here: 1300 us
  waiting for transfers between devices  725 us (55%)
  other arithmetic  275 us (21%)
  local copies, waits for them, and re-layouts  132 us (10%)
  matrix products  103 us (8%)
  blocking collectives  40 us (3%)
  between operations  19.4 us (1%)
    all_to_all x1, waiting for transfers between devices, on_device(): lax.all_to_all(every_part, 'col', split_axis=0, concat_axis=1, tiled=True)  378 us
    all_gather x1, waiting for transfers between devices, on_device(): lax.all_gather(row_part, 'col', axis=1, tiled=True)  227 us
    another operation x30, other arithmetic, on_device(): factor = jnp.linalg.cholesky(gathered)  173 us
    another operation x3, other arithmetic, on_device(): lax.linalg.triangular_solve(factor, coupling, left_side=False, lower=True...  87.1 us
    all_gather x1, waiting for transfers between devices, on_device(): gathered = lax.all_gather(diag_blocks, 'col', axis=1, tiled=True)  72.7 us
    dot_general x1, matrix products, on_device(): lax.dot_general(lax.all_gather(row_part, 'col', axis=1, tiled=True), col_...  48.9 us
    all_gather x1, waiting for transfers between devices, on_device(): panel_slab = lax.all_gather(panel_tiles, 'grp', axis=0, tiled=True)  47.8 us
    all_to_all x1, blocking collectives, on_device(): lax.all_to_all(panel_half, 'col', split_axis=1, concat_axis=0, tiled=True)  40 us
  transfers between devices with their start and end apart: 4, of which 4 were waited for; matrix products, arithmetic and copies ran while one was open for 1% of the time, Pallas kernels for 0%

commit v1 on v0

--- a/solution.py
+++ b/solution.py
@@ -1,12 +1,20 @@
+import functools
+
 import jax
 import jax.numpy as jnp
 from jax import lax
+from jax.experimental import pallas as pl
+from jax.experimental.pallas import tpu as pltpu
 from jax.sharding import PartitionSpec as P
 
 FRONTS = 4
 BLK = 128
 SBLK = 48
 PBLK = 96
+F32 = jnp.float32
+HALF = jnp.bfloat16
+EXACT = lax.Precision.HIGHEST
+ANY = pl.BlockSpec(memory_space=pl.ANY)
 
 
 def swapped(block, axis, stride):
@@ -25,7 +33,7 @@
     return jnp.transpose(picked, (1, 2, 0, 3)).reshape(count * BLK, -1)
 
 
-def on_device(diag_blocks, coupling, parent_front, index_maps):
+def general(diag_blocks, coupling, parent_front, index_maps):
     groups = lax.axis_size("grp") // FRONTS
     swap_depth = groups.bit_length() - 1
     grp_index = lax.axis_index("grp")
@@ -47,7 +55,7 @@
     panel_rows = lax.linalg.triangular_solve(
         factor, coupling, left_side=False, lower=True, transpose_a=True
     )
-    panel_half = panel_rows.astype(jnp.bfloat16)
+    panel_half = panel_rows.astype(HALF)
     panel_tiles = lax.all_to_all(panel_half, "col", split_axis=1, concat_axis=0, tiled=True)
     panel_slab = lax.all_gather(panel_tiles, "grp", axis=0, tiled=True)
     slab_blocks = panel_slab.reshape(FRONTS, SBLK, BLK, -1)
@@ -64,10 +72,376 @@
         lax.all_gather(row_part, "col", axis=1, tiled=True),
         col_operand,
         contract,
-        preferred_element_type=jnp.float32,
-    )
-    merged = parent_front - update
-    return (merged, factor_tile, panel_rows)
+        preferred_element_type=F32,
+    )
+    return (parent_front - update, factor_tile, panel_rows)
+
+
+def dot(a, b, ca, cb):
+    return lax.dot_general(
+        a, b, (((ca,), (cb,)), ((), ())), precision=EXACT, preferred_element_type=F32
+    )
+
+
+def eliminate(s_val, u_ref, inv_ref, width):
+    rows = 8
+    shape = (width, width)
+    eye = lax.broadcasted_iota(jnp.int32, shape, 0) == lax.broadcasted_iota(jnp.int32, shape, 1)
+    sub = lax.broadcasted_iota(jnp.int32, (rows, 1), 0)
+
+    def group(g, carry):
+        s, e = carry
+        scale = jnp.zeros((rows, 1), F32)
+        for i in range(rows):
+            pivot = s[i : i + 1, i : i + 1]
+            s_row, e_row = s[i : i + 1, :], e[i : i + 1, :]
+            mult = s[:, i : i + 1] * (1.0 / pivot)
+            below = jnp.where(sub > i, mult[:rows], 0.0)
+            mult = jnp.concatenate([below, mult[rows:]], axis=0)
+            s = s - mult * s_row
+            e = e - mult * e_row
+            scale = jnp.where(sub == i, lax.rsqrt(pivot), scale)
+        at = pl.multiple_of(g * rows, rows)
+        u_ref[pl.ds(at, rows), :] = pltpu.roll(s[:rows] * scale, at, 1)
+        inv_ref[pl.ds(at, rows), :] = e[:rows] * scale
+        s = jnp.concatenate([s[rows:], s[:rows]], axis=0)
+        e = jnp.concatenate([e[rows:], e[:rows]], axis=0)
+        return pltpu.roll(s, width - rows, 1), e
+
+    lax.fori_loop(0, width // rows, group, (s_val, eye.astype(F32)))
+
+
+def factor_body(k, width, cols, col_ref, *refs):
+    pieces, c_ref, refs = refs[:cols], refs[cols], refs[cols + 1 :]
+    if k:
+        u_in, x_in, refs = refs[0], refs[1], refs[2:]
+    u_out, x_out, half_ref, u_v, x_v, s_v, t_v, uk_v, inv_v, sem = refs
+    n = s_v.shape[1]
+    base = k * width
+    rest = n - base - width
+    here = pl.ds(base, width)
+    if k:
+        before = pl.ds(0, base)
+        load_u = pltpu.make_async_copy(u_in.at[before, :], u_v.at[before, :], sem.at[0])
+        load_x = pltpu.make_async_copy(x_in.at[:, before], x_v.at[:, before], sem.at[1])
+        load_u.start()
+        load_x.start()
+    for rel in range(cols):
+        at = pl.multiple_of((col_ref[0] ^ rel) * width, width)
+        s_v[:, pl.ds(at, width)] = pieces[rel][...]
+    if k:
+        load_u.wait()
+
+        def prev(j, _):
+            at = pl.multiple_of(j * width, width)
+            uj = u_v[pl.ds(at, width), pl.ds(base, n - base)]
+            s_v[:, pl.ds(base, n - base)] -= dot(uj[:, :width], uj, 0, 0)
+            return 0
+
+        lax.fori_loop(0, k, prev, 0)
+    eliminate(s_v[:, here], uk_v, inv_v, width)
+    inv = inv_v[...]
+    r = lax.broadcasted_iota(jnp.int32, (width, width), 0)
+    c = lax.broadcasted_iota(jnp.int32, (width, width), 1)
+    if base:
+        u_v[here, pl.ds(0, base)] = jnp.zeros((width, base), F32)
+    u_v[here, here] = jnp.where(c >= r, uk_v[...], 0.0)
+    if rest:
+        right = pl.ds(base + width, rest)
+        u_v[here, right] = dot(inv, s_v[:, right], 1, 0)
+    save_u = pltpu.make_async_copy(u_v.at[here, :], u_out.at[here, :], sem.at[2])
+    save_u.start()
+    t_v[...] = c_ref[...]
+    if k:
+        load_x.wait()
+
+        def prevx(j, _):
+            at = pl.multiple_of(j * width, width)
+            t_v[...] -= dot(x_v[:, pl.ds(at, width)], u_v[pl.ds(at, width), here], 1, 0)
+            return 0
+
+        lax.fori_loop(0, k, prevx, 0)
+    x_v[:, here] = dot(t_v[...], inv, 1, 1)
+    half_ref[...] = x_v[:, here].astype(HALF)
+    save_x = pltpu.make_async_copy(x_v.at[:, here], x_out.at[:, here], sem.at[3])
+    save_x.start()
+    save_u.wait()
+    save_x.wait()
+
+
+def factor_step(k, first, pieces, coupling, u_all, x_all, col_id):
+    m, n = coupling.shape
+    width = pieces[0].shape[1]
+    cols = len(pieces)
+    args = [*pieces, coupling]
+    specs = [pl.BlockSpec((width, width), lambda i, s: (k - first, 0))] * cols
+    specs += [pl.BlockSpec((m, width), lambda i, s: (0, k))]
+    alias = {}
+    if k:
+        alias = {len(args) + 1: 0, len(args) + 2: 1}
+        args += [u_all, x_all]
+        specs += [ANY, ANY]
+    square = pltpu.VMEM((width, width), F32)
+    return pl.pallas_call(
+        functools.partial(factor_body, k, width, cols),
+        grid_spec=pltpu.PrefetchScalarGridSpec(
+            num_scalar_prefetch=1,
+            grid=(1,),
+            in_specs=specs,
+            out_specs=(ANY, ANY, pl.BlockSpec((m, width), lambda i, s: (0, 0))),
+            scratch_shapes=[
+                pltpu.VMEM((n, n), F32),
+                pltpu.VMEM((m, n), F32),
+                pltpu.VMEM((width, n), F32),
+                pltpu.VMEM((m, width), F32),
+                square,
+                square,
+                pltpu.SemaphoreType.DMA((4,)),
+            ],
+        ),
+        out_shape=(
+            jax.ShapeDtypeStruct((n, n), F32),
+            jax.ShapeDtypeStruct((m, n), F32),
+            jax.ShapeDtypeStruct((m, width), HALF),
+        ),
+        input_output_aliases=alias,
+        compiler_params=pltpu.CompilerParams(vmem_limit_bytes=32 << 20),
+        cost_estimate=pl.CostEstimate(
+            flops=10**9, bytes_accessed=48 << 20, transcendentals=0
+        ),
+        name=f"factor{k}",
+    )(col_id, *args)
+
+
+def extend_body(count, per, split, maps, place, parent, *refs):
+    arrays, refs = refs[: count * split], refs[count * split :]
+    out, acc, lhs, rhs, lists, sem, acc_sem = refs
+    rows, cols = parent.shape
+    nrb, ncb = rows // BLK, cols // BLK
+    width = arrays[0].shape[1]
+    load = pltpu.make_async_copy(parent, acc, acc_sem.at[0])
+    load.start()
+    grp, col, zs = place[0], place[1], place[2]
+    x_at, core_at = grp // 2, grp % 2
+
+    def locate(f, i):
+        src = i // per
+        dc = (f % 2) ^ core_at
+        dx = (f // 2) ^ x_at
+        dcol = src ^ col
+        dy = dcol % 2
+        dz = dcol // 2
+        near = jnp.where((core_at ^ dc) == 0, dx + 2 * dy, dy + 2 * dx)
+        return 4 * dc + near, (dz * per + i % per) * BLK
+
+    def fetch(f, slot):
+        def scan(i, state):
+            nr, nc = state
+            p = maps[f, i]
+            which, start = locate(f, i)
+            start = pl.multiple_of(start, BLK)
+            in_rows = p // nrb == grp
+            in_cols = p // ncb == col
+
+            @pl.when(in_rows)
+            def _():
+                lists[slot, nr] = p % nrb
+
+            @pl.when(in_cols)
+            def _():
+                lists[slot, nrb + nc] = p % ncb
+
+            @pl.when(in_rows | in_cols)
+            def _():
+                for a in range(split):
+
+                    @pl.when(which == a)
+                    def _():
+                        for n in range(count):
+                            src = arrays[n * split + a].at[pl.ds(start, BLK), :]
+                            where = pl.ds(n * width, width)
+
+                            @pl.when(in_rows)
+                            def _():
+                                at = pl.ds(pl.multiple_of(nr * BLK, BLK), BLK)
+                                pltpu.make_async_copy(
+                                    src, lhs.at[slot, at, where], sem.at[slot]
+                                ).start()
+
+                            @pl.when(in_cols)
+                            def _():
+                                at = pl.ds(pl.multiple_of(nc * BLK, BLK), BLK)
+                                pltpu.make_async_copy(
+                                    src, rhs.at[slot, at, where], sem.at[slot]
+                                ).start()
+
+            return nr + in_rows.astype(jnp.int32), nc + in_cols.astype(jnp.int32)
+
+        zero = jnp.int32(0)
+        nr, nc = lax.fori_loop(0, maps.shape[1], scan, (zero, zero))
+        lists[slot, nrb + ncb] = nr
+        lists[slot, nrb + ncb + 1] = nc
+
+    def drain(slot):
+        total = lists[slot, nrb + ncb] + lists[slot, nrb + ncb + 1]
+
+        def one(_, carry):
+            block = lhs.at[slot, pl.ds(0, BLK), :]
+            pltpu.make_async_copy(block, block, sem.at[slot]).wait()
+            return carry
+
+        lax.fori_loop(0, total, one, 0)
+
+    fetch(0, 0)
+    for f in range(FRONTS):
+        slot = f % 2
+        if f + 1 < FRONTS:
+            fetch(f + 1, 1 - slot)
+        drain(slot)
+        if f == 0:
+            load.wait()
+        nr, nc = lists[slot, nrb + ncb], lists[slot, nrb + ncb + 1]
+        tall, wide = 4, 2
+
+        def col_step(j, _):
+            right = rhs[slot, pl.ds(pl.multiple_of(j * wide * BLK, wide * BLK), wide * BLK), :]
+
+            def row_step(i, _):
+                left = lhs[slot, pl.ds(pl.multiple_of(i * tall * BLK, tall * BLK), tall * BLK), :]
+                prod = lax.dot_general(
+                    left, right, (((1,), (1,)), ((), ())), preferred_element_type=F32
+                )
+                for b in range(wide):
+                    for a in range(tall):
+
+                        @pl.when((i * tall + a < nr) & (j * wide + b < nc))
+                        def _():
+                            r = pl.multiple_of(lists[slot, i * tall + a] * BLK, BLK)
+                            c = pl.multiple_of(lists[slot, nrb + j * wide + b] * BLK, BLK)
+                            acc[pl.ds(r, BLK), pl.ds(c, BLK)] -= prod[
+                                a * BLK : (a + 1) * BLK, b * BLK : (b + 1) * BLK
+                            ]
+
+                return 0
+
+            lax.fori_loop(0, (nr + tall - 1) // tall, row_step, 0)
+            return 0
+
+        lax.fori_loop(0, (nc + wide - 1) // wide, col_step, 0)
+    store = pltpu.make_async_copy(acc, out, acc_sem.at[1])
+    store.start()
+    store.wait()
+
+
+def extend_add(parent, chunks, index_maps, place, per):
+    count, split = len(chunks), len(chunks[0])
+    rows, cols = parent.shape
+    nrb, ncb = rows // BLK, cols // BLK
+    depth = sum(chunk[0].shape[1] for chunk in chunks)
+    even = 4 * BLK
+    return pl.pallas_call(
+        functools.partial(extend_body, count, per, split),
+        grid_spec=pltpu.PrefetchScalarGridSpec(
+            num_scalar_prefetch=2,
+            grid=(1,),
+            in_specs=[ANY] * (1 + count * split),
+            out_specs=ANY,
+            scratch_shapes=[
+                pltpu.VMEM((rows, cols), F32),
+                pltpu.VMEM((2, -(-rows // even) * even, depth), HALF),
+                pltpu.VMEM((2, -(-cols // even) * even, depth), HALF),
+                pltpu.SMEM((2, nrb + ncb + 2), jnp.int32),
+                pltpu.SemaphoreType.DMA((2,)),
+                pltpu.SemaphoreType.DMA((2,)),
+            ],
+        ),
+        out_shape=jax.ShapeDtypeStruct((rows, cols), F32),
+        compiler_params=pltpu.CompilerParams(vmem_limit_bytes=58 << 20),
+        cost_estimate=pl.CostEstimate(
+            flops=2 * rows * cols * depth, bytes_accessed=64 << 20, transcendentals=0
+        ),
+        name="extend_add",
+    )(index_maps, place, parent, *[a for chunk in chunks for a in chunk])
+
+
+def paired(size_grp, size_col, flip):
+    route = []
+    for g in range(size_grp):
+        for c in range(size_col):
+            to = flip(g, c)
+            if to is not None:
+                route.append((g * size_col + c, to[0] * size_col + to[1]))
+    return route
+
+
+def fronts_apart(diag_blocks, coupling, parent_front, index_maps):
+    ng, nc = lax.axis_size("grp"), lax.axis_size("col")
+    nz = nc // 2
+    grp, col = lax.axis_index("grp"), lax.axis_index("col")
+    width = diag_blocks.shape[1]
+    blocks = coupling.shape[1] // width
+    per = coupling.shape[0] // BLK
+
+    def send(block, flip):
+        return lax.ppermute(block, ("grp", "col"), paired(ng, nc, flip))
+
+    def gather_rows(first, last):
+        own = lax.slice_in_dim(diag_blocks, first * width, last * width, axis=0)
+        along = [own]
+        for dz in range(1, nz):
+            along.append(send(own, lambda g, c: (g, c ^ 2 * dz) if c >= first else None))
+        out = []
+        for dz in range(nz):
+            across = send(
+                along[dz], lambda g, c: (g, c ^ 1) if c ^ 2 * dz >= first else None
+            )
+            out += [along[dz], across]
+        return out
+
+    cuts = [0, 1, 3, blocks]
+    pieces = {}
+    for first, last in zip(cuts, cuts[1:]):
+        got = gather_rows(first, last)
+        for k in range(first, last):
+            pieces[k] = (first, got)
+
+    col_id = jnp.reshape(col, (1,)).astype(jnp.int32)
+    place = jnp.stack([grp, col, jnp.int32(nz)]).astype(jnp.int32)
+    u_all = x_all = None
+    chunks = []
+    for k in range(blocks):
+        first, got = pieces[k]
+        u_all, x_all, half = factor_step(k, first, got, coupling, u_all, x_all, col_id)
+        line = [half] + [send(half, lambda g, c: (g, c ^ 2 * dz)) for dz in range(1, nz)]
+        own = jnp.concatenate(line, axis=0)
+
+        def one_way(g, c):
+            return (g ^ 2, c) if g % 2 == 0 else (g, c ^ 1)
+
+        def other_way(g, c):
+            return (g, c ^ 1) if g % 2 == 0 else (g ^ 2, c)
+
+        side = send(own, one_way)
+        here = [own, side, send(own, other_way), send(side, other_way)]
+        there = [send(a, lambda g, c: (g ^ 1, c)) for a in here]
+        chunks.append(here + there)
+
+    merged = extend_add(parent_front, chunks, index_maps, place, per)
+    mine = lax.dynamic_slice_in_dim(u_all, col * width, width, 0)
+    return (merged, mine.T, x_all)
+
+
+def on_device(diag_blocks, coupling, parent_front, index_maps):
+    ng, nc = lax.axis_size("grp"), lax.axis_size("col")
+    simple = (
+        ng == FRONTS
+        and nc % 2 == 0
+        and nc & (nc - 1) == 0
+        and diag_blocks.shape[1] == BLK
+        and coupling.shape[0] % BLK == 0
+    )
+    body = fronts_apart if simple else general
+    return body(diag_blocks, coupling, parent_front, index_maps)
 
 
 def solution(mesh):

time: 1310 us -> 544 us (0.42)
  the two profiles are of different devices: /device:TPU:29 before, /device:TPU:22 now
where the time goes in v1:
time: 544 us; the launch traced here: 543 us
  waiting for transfers between devices  241 us (44%)
  Pallas kernels  189 us (35%)
  starting transfers between devices  102 us (19%)
  local copies, waits for them, and re-layouts  9.24 us (2%)
    ppermute x101, waiting for transfers between devices, send(): return lax.ppermute(block, ('grp', 'col'), paired(ng, nc, flip))  241 us
    pallas_call x8, Pallas kernels, factor_step(): pl.pallas_call(functools.partial(factor_body, k, width, cols), grid_spec=...  133 us
    ppermute x101, starting transfers between devices, send(): return lax.ppermute(block, ('grp', 'col'), paired(ng, nc, flip))  102 us
    pallas_call x1, Pallas kernels, extend_add(): pl.pallas_call(functools.partial(extend_body, count, per, split), grid_sp...  55.4 us
  transfers between devices with their start and end apart: 101, of which 38 were waited for; matrix products, arithmetic and copies ran while one was open for 1% of the time, Pallas kernels for 25%

profile of v1, /device:TPU:22, one launch (start us, length us, event | category | flops | bytes accessed | tf_op | source)
XLA Modules:
  0.0 543.0 jit_solution(11599208007479362580)
XLA Ops:
  47.1 13.7 %factor0.1 = (f32[1024,1024]{1,0:T(8,128)S(1)}, f32[768,1024]{1,0:T(8,128)}, bf16[768,128]{1,0:T(8,128)(2,1)S(1)}) custom-call(s32[1]{0:T(128)} %bitcast.1.col_ref, f32[128,128]{1,0:T(8,128)S(1)} %slice.9.refs_0_, f32[128,128]{1,0:T(8,128)S(1)} %collective-permute-done.refs_1_, f32[128,128]{1,0:T(8,128)S(1)} %collective-permute-done.1.refs_2_, ...), custom_call_target="tpu_custom_call" | custom-call | flops 1000000000 | bytes 50331648 | tf_op jit(solution)/shard_map/factor0/pallas_call | solution.py:185
  64.2 15.3 %factor1.1 = (f32[1024,1024]{1,0:T(8,128)S(1)}, f32[768,1024]{1,0:T(8,128)}, bf16[768,128]{1,0:T(8,128)(2,1)S(1)}) custom-call(s32[1]{0:T(128)} %bitcast.1.col_ref, f32[256,128]{1,0:T(8,128)S(1)} %slice.10.refs_0_, f32[256,128]{1,0:T(8,128)S(1)} %collective-permute-done.17.refs_1_, ...), custom_call_target="tpu_custom_call", output_to_operand_aliasing={{0}: (10, {}), {1}: (11, {})} | custom-call | flops 1000000000 | bytes 50331648 | tf_op jit(solution)/shard_map/factor1/pallas_call | solution.py:185
  85.6 15.6 %factor2.1 = (f32[1024,1024]{1,0:T(8,128)S(1)}, f32[768,1024]{1,0:T(8,128)}, bf16[768,128]{1,0:T(8,128)(2,1)S(1)}) custom-call(s32[1]{0:T(128)} %bitcast.1.col_ref, f32[256,128]{1,0:T(8,128)S(1)} %slice.10.refs_0_, f32[256,128]{1,0:T(8,128)S(1)} %collective-permute-done.17.refs_1_, ...), custom_call_target="tpu_custom_call", output_to_operand_aliasing={{0}: (10, {}), {1}: (11, {})} | custom-call | flops 1000000000 | bytes 50331648 | tf_op jit(solution)/shard_map/factor2/pallas_call | solution.py:185
  112.1 16.5 %factor3.1 = (f32[1024,1024]{1,0:T(8,128)S(1)}, f32[768,1024]{1,0:T(8,128)}, bf16[768,128]{1,0:T(8,128)(2,1)S(1)}) custom-call(s32[1]{0:T(128)} %bitcast.1.col_ref, f32[640,128]{1,0:T(8,128)S(1)} %slice.11.refs_0_, f32[640,128]{1,0:T(8,128)S(1)} %collective-permute-done.44.refs_1_, ...), custom_call_target="tpu_custom_call", output_to_operand_aliasing={{0}: (10, {}), {1}: (11, {})} | custom-call | flops 1000000000 | bytes 50331648 | tf_op jit(solution)/shard_map/factor3/pallas_call | solution.py:185
  128.5 17.1 %factor4.1 = (f32[1024,1024]{1,0:T(8,128)S(1)}, f32[768,1024]{1,0:T(8,128)}, bf16[768,128]{1,0:T(8,128)(2,1)S(1)}) custom-call(s32[1]{0:T(128)} %bitcast.1.col_ref, f32[640,128]{1,0:T(8,128)S(1)} %slice.11.refs_0_, f32[640,128]{1,0:T(8,128)S(1)} %collective-permute-done.44.refs_1_, ...), custom_call_target="tpu_custom_call", output_to_operand_aliasing={{0}: (10, {}), {1}: (11, {})} | custom-call | flops 1000000000 | bytes 50331648 | tf_op jit(solution)/shard_map/factor4/pallas_call | solution.py:185
  145.7 17.8 %factor5.1 = (f32[1024,1024]{1,0:T(8,128)S(1)}, f32[768,1024]{1,0:T(8,128)}, bf16[768,128]{1,0:T(8,128)(2,1)S(1)}) custom-call(s32[1]{0:T(128)} %bitcast.1.col_ref, f32[640,128]{1,0:T(8,128)S(1)} %slice.11.refs_0_, f32[640,128]{1,0:T(8,128)S(1)} %collective-permute-done.44.refs_1_, ...), custom_call_target="tpu_custom_call", output_to_operand_aliasing={{0}: (10, {}), {1}: (11, {})} | custom-call | flops 1000000000 | bytes 50331648 | tf_op jit(solution)/shard_map/factor5/pallas_call | solution.py:185
  163.5 18.3 %factor6.1 = (f32[1024,1024]{1,0:T(8,128)S(1)}, f32[768,1024]{1,0:T(8,128)}, bf16[768,128]{1,0:T(8,128)(2,1)S(1)}) custom-call(s32[1]{0:T(128)} %bitcast.1.col_ref, f32[640,128]{1,0:T(8,128)S(1)} %slice.11.refs_0_, f32[640,128]{1,0:T(8,128)S(1)} %collective-permute-done.44.refs_1_, ...), custom_call_target="tpu_custom_call", output_to_operand_aliasing={{0}: (10, {}), {1}: (11, {})} | custom-call | flops 1000000000 | bytes 50331648 | tf_op jit(solution)/shard_map/factor6/pallas_call | solution.py:185
  185.7 18.8 %factor7.1 = (f32[1024,1024]{1,0:T(8,128)S(1)}, f32[768,1024]{1,0:T(8,128)}, bf16[768,128]{1,0:T(8,128)(2,1)S(1)}) custom-call(s32[1]{0:T(128)} %bitcast.1.col_ref, f32[640,128]{1,0:T(8,128)S(1)} %slice.11.refs_0_, f32[640,128]{1,0:T(8,128)S(1)} %collective-permute-done.44.refs_1_, ...), custom_call_target="tpu_custom_call", output_to_operand_aliasing={{0}: (10, {}), {1}: (11, {})} | custom-call | flops 1000000000 | bytes 50331648 | tf_op jit(solution)/shard_map/factor7/pallas_call | solution.py:185
  223.1 7.8 %collective-permute-start.81 = (bf16[768,128]{1,0:T(8,128)(2,1)S(1)}, bf16[768,128]{1,0:T(8,128)(2,1)S(1)}, u32[]{:S(2)}, u32[]{:S(2)}) collective-permute-start(bf16[768,128]{1,0:T(8,128)(2,1)S(1)} %get-tuple-element.45), channel_id=1, source_target_pairs={{0,2},{1,3},{2,0},{3,1},{4,6},{5,7},{6,4},{7,5},{8,10},{9,11},{10,... | collective-permute-start | bytes 589832 | tf_op jit(solution)/shard_map/ppermute | solution.py:386
  230.9 7.6 %collective-permute-done.83 = bf16[768,128]{1,0:T(8,128)(2,1)S(1)} collective-permute-done((bf16[768,128]{1,0:T(8,128)(2,1)S(1)}, bf16[768,128]{1,0:T(8,128)(2,1)S(1)}, u32[]{:S(2)}, u32[]{:S(2)}) %collective-permute-start.83) | collective-permute-done | bytes 196640 | tf_op jit(solution)/shard_map/ppermute | solution.py:386
  245.4 10.0 %collective-permute-done.73 = bf16[768,128]{1,0:T(8,128)(2,1)S(1)} collective-permute-done((bf16[768,128]{1,0:T(8,128)(2,1)S(1)}, bf16[768,128]{1,0:T(8,128)(2,1)S(1)}, u32[]{:S(2)}, u32[]{:S(2)}) %collective-permute-start.73) | collective-permute-done | bytes 196640 | tf_op jit(solution)/shard_map/ppermute | solution.py:386
  262.3 10.0 %collective-permute-done.63 = bf16[768,128]{1,0:T(8,128)(2,1)S(1)} collective-permute-done((bf16[768,128]{1,0:T(8,128)(2,1)S(1)}, bf16[768,128]{1,0:T(8,128)(2,1)S(1)}, u32[]{:S(2)}, u32[]{:S(2)}) %collective-permute-start.63) | collective-permute-done | bytes 196640 | tf_op jit(solution)/shard_map/ppermute | solution.py:386
  285.5 13.0 %collective-permute-done.11.refs_2_ = bf16[3072,128]{1,0:T(8,128)(2,1)S(1)} collective-permute-done((bf16[3072,128]{1,0:T(8,128)(2,1)S(1)}, bf16[3072,128]{1,0:T(8,128)(2,1)S(1)}, u32[]{:S(2)}, u32[]{:S(2)}) %collective-permute-start.11) | collective-permute-done | bytes 786464 | tf_op jit(solution)/shard_map/ppermute | solution.py:386
  302.8 12.5 %collective-permute-done.28.refs_10_ = bf16[3072,128]{1,0:T(8,128)(2,1)S(1)} collective-permute-done((bf16[3072,128]{1,0:T(8,128)(2,1)S(1)}, bf16[3072,128]{1,0:T(8,128)(2,1)S(1)}, u32[]{:S(2)}, u32[]{:S(2)}) %collective-permute-start.28) | collective-permute-done | bytes 786464 | tf_op jit(solution)/shard_map/ppermute | solution.py:386
  320.0 12.3 %collective-permute-done.38.refs_18_ = bf16[3072,128]{1,0:T(8,128)(2,1)S(1)} collective-permute-done((bf16[3072,128]{1,0:T(8,128)(2,1)S(1)}, bf16[3072,128]{1,0:T(8,128)(2,1)S(1)}, u32[]{:S(2)}, u32[]{:S(2)}) %collective-permute-start.38) | collective-permute-done | bytes 786464 | tf_op jit(solution)/shard_map/ppermute | solution.py:386
  336.5 12.5 %collective-permute-done.55.refs_26_ = bf16[3072,128]{1,0:T(8,128)(2,1)S(1)} collective-permute-done((bf16[3072,128]{1,0:T(8,128)(2,1)S(1)}, bf16[3072,128]{1,0:T(8,128)(2,1)S(1)}, u32[]{:S(2)}, u32[]{:S(2)}) %collective-permute-start.55) | collective-permute-done | bytes 786464 | tf_op jit(solution)/shard_map/ppermute | solution.py:386
  353.4 12.5 %collective-permute-done.65.refs_34_ = bf16[3072,128]{1,0:T(8,128)(2,1)S(1)} collective-permute-done((bf16[3072,128]{1,0:T(8,128)(2,1)S(1)}, bf16[3072,128]{1,0:T(8,128)(2,1)S(1)}, u32[]{:S(2)}, u32[]{:S(2)}) %collective-permute-start.65) | collective-permute-done | bytes 786464 | tf_op jit(solution)/shard_map/ppermute | solution.py:386
  370.4 12.4 %collective-permute-done.75.refs_42_ = bf16[3072,128]{1,0:T(8,128)(2,1)S(1)} collective-permute-done((bf16[3072,128]{1,0:T(8,128)(2,1)S(1)}, bf16[3072,128]{1,0:T(8,128)(2,1)S(1)}, u32[]{:S(2)}, u32[]{:S(2)}) %collective-permute-start.75) | collective-permute-done | bytes 786464 | tf_op jit(solution)/shard_map/ppermute | solution.py:386
  387.1 12.5 %collective-permute-done.85.refs_50_ = bf16[3072,128]{1,0:T(8,128)(2,1)S(1)} collective-permute-done((bf16[3072,128]{1,0:T(8,128)(2,1)S(1)}, bf16[3072,128]{1,0:T(8,128)(2,1)S(1)}, u32[]{:S(2)}, u32[]{:S(2)}) %collective-permute-start.85) | collective-permute-done | bytes 786464 | tf_op jit(solution)/shard_map/ppermute | solution.py:386
  404.0 9.8 %collective-permute-done.95.refs_58_ = bf16[3072,128]{1,0:T(8,128)(2,1)S(1)} collective-permute-done((bf16[3072,128]{1,0:T(8,128)(2,1)S(1)}, bf16[3072,128]{1,0:T(8,128)(2,1)S(1)}, u32[]{:S(2)}, u32[]{:S(2)}) %collective-permute-start.95) | collective-permute-done | bytes 786464 | tf_op jit(solution)/shard_map/ppermute | solution.py:386
  423.0 7.7 %collective-permute-done.29.refs_11_ = bf16[3072,128]{1,0:T(8,128)(2,1)S(1)} collective-permute-done((bf16[3072,128]{1,0:T(8,128)(2,1)S(1)}, bf16[3072,128]{1,0:T(8,128)(2,1)S(1)}, u32[]{:S(2)}, u32[]{:S(2)}) %collective-permute-start.29) | collective-permute-done | bytes 786464 | tf_op jit(solution)/shard_map/ppermute | solution.py:386
  440.3 7.4 %collective-permute-done.56.refs_27_ = bf16[3072,128]{1,0:T(8,128)(2,1)} collective-permute-done((bf16[3072,128]{1,0:T(8,128)(2,1)S(1)}, bf16[3072,128]{1,0:T(8,128)(2,1)}, u32[]{:S(2)}, u32[]{:S(2)}) %collective-permute-start.56) | collective-permute-done | bytes 786464 | tf_op jit(solution)/shard_map/ppermute | solution.py:386
  473.6 7.7 %collective-permute-done.96.refs_59_ = bf16[3072,128]{1,0:T(8,128)(2,1)} collective-permute-done((bf16[3072,128]{1,0:T(8,128)(2,1)S(1)}, bf16[3072,128]{1,0:T(8,128)(2,1)}, u32[]{:S(2)}, u32[]{:S(2)}) %collective-permute-start.96) | collective-permute-done | bytes 786464 | tf_op jit(solution)/shard_map/ppermute | solution.py:386
  487.4 55.4 %extend_add.1 = f32[3072,1536]{1,0:T(8,128)} custom-call(s32[4,48]{1,0:T(4,128)} %maps.1, s32[3]{0:T(128)} %pad_add_fusion.place, f32[3072,1536]{1,0:T(8,128)} %parent.1, bf16[3072,128]{1,0:T(8,128)(2,1)} %copy-done.2, bf16[3072,128]{1,0:T(8,128)(2,1)} %copy-done.12, bf16[3072,128]{1,0:T(8,128)(2,1)} %copy-done.11, bf16[3072,128]{1,0:T(8,128)(2,1)} %copy-done.36, ...), custom_call_target="tpu_custom_call" | custom-call | flops 9663676416 | bytes 67108864 | tf_op jit(solution)/shard_map/extend_add/pallas_call | solution.py:342
  (337 shorter events, 196.4 us)
Async XLA Ops:
  29.7 31.2 %collective-permute-start.21 = (f32[256,128]{1,0:T(8,128)S(1)}, f32[256,128]{1,0:T(8,128)S(1)}, u32[]{:S(2)}, u32[]{:S(2)}) collective-permute-start(f32[256,128]{1,0:T(8,128)S(1)} %collective-permute-done.20.refs_4_), channel_id=1, source_target_pairs={{0,1},{1,0},{2,3},{3,2},{5,4},{6,7},{7,6},{8,9},{9,8},{10,11},{11,... | collective-permute-start | bytes 393224 | tf_op jit(solution)/shard_map/ppermute | solution.py:386
  33.3 46.2 %collective-permute-start.49 = (f32[640,128]{1,0:T(8,128)S(1)}, f32[640,128]{1,0:T(8,128)S(1)}, u32[]{:S(2)}, u32[]{:S(2)}) collective-permute-start(f32[640,128]{1,0:T(8,128)S(1)} %slice.11.refs_0_), channel_id=1, source_target_pairs={{3,5},{4,2},{5,3},{6,0},{7,1},{11,13},{12,10},{13,11},{14,8},{15,9... | collective-permute-start | bytes 983048 | tf_op jit(solution)/shard_map/ppermute | solution.py:386
  37.3 42.3 %collective-permute-start.47 = (f32[640,128]{1,0:T(8,128)S(1)}, f32[640,128]{1,0:T(8,128)S(1)}, u32[]{:S(2)}, u32[]{:S(2)}) collective-permute-start(f32[640,128]{1,0:T(8,128)S(1)} %slice.11.refs_0_), channel_id=1, source_target_pairs={{3,7},{4,0},{5,1},{6,2},{7,3},{11,15},{12,8},{13,9},{14,10},{15,11... | collective-permute-start | bytes 983048 | tf_op jit(solution)/shard_map/ppermute | solution.py:386
  38.6 44.2 %collective-permute-start.45 = (f32[640,128]{1,0:T(8,128)S(1)}, f32[640,128]{1,0:T(8,128)S(1)}, u32[]{:S(2)}, u32[]{:S(2)}) collective-permute-start(f32[640,128]{1,0:T(8,128)S(1)} %slice.11.refs_0_), channel_id=1, source_target_pairs={{3,1},{4,6},{5,7},{6,4},{7,5},{11,9},{12,14},{13,15},{14,12},{15,1... | collective-permute-start | bytes 983048 | tf_op jit(solution)/shard_map/ppermute | solution.py:386
  61.5 44.0 %collective-permute-start.44 = (f32[640,128]{1,0:T(8,128)S(1)}, f32[640,128]{1,0:T(8,128)S(1)}, u32[]{:S(2)}, u32[]{:S(2)}) collective-permute-start(f32[640,128]{1,0:T(8,128)S(1)} %slice.11.refs_0_), channel_id=1, source_target_pairs={{3,2},{4,5},{5,4},{6,7},{7,6},{11,10},{12,13},{13,12},{14,15},{15,... | collective-permute-start | bytes 983048 | tf_op jit(solution)/shard_map/ppermute | solution.py:386
  101.3 80.5 %collective-permute-start.9 = (bf16[768,128]{1,0:T(8,128)(2,1)S(1)}, bf16[768,128]{1,0:T(8,128)(2,1)S(1)}, u32[]{:S(2)}, u32[]{:S(2)}) collective-permute-start(bf16[768,128]{1,0:T(8,128)(2,1)S(1)} %get-tuple-element.27), channel_id=1, source_target_pairs={{0,6},{1,7},{2,4},{3,5},{4,2},{5,3},{6,0},{7,1},{8,14},{9,15},{10,... | collective-permute-start | bytes 589832 | tf_op jit(solution)/shard_map/ppermute | solution.py:386
  105.6 98.9 %collective-permute-start.36 = (bf16[768,128]{1,0:T(8,128)(2,1)S(1)}, bf16[768,128]{1,0:T(8,128)(2,1)S(1)}, u32[]{:S(2)}, u32[]{:S(2)}) collective-permute-start(bf16[768,128]{1,0:T(8,128)(2,1)S(1)} %get-tuple-element.33), channel_id=1, source_target_pairs={{0,6},{1,7},{2,4},{3,5},{4,2},{5,3},{6,0},{7,1},{8,14},{9,15},{10,... | collective-permute-start | bytes 589832 | tf_op jit(solution)/shard_map/ppermute | solution.py:386
  105.7 98.9 %collective-permute-start.35 = (bf16[768,128]{1,0:T(8,128)(2,1)S(1)}, bf16[768,128]{1,0:T(8,128)(2,1)S(1)}, u32[]{:S(2)}, u32[]{:S(2)}) collective-permute-start(bf16[768,128]{1,0:T(8,128)(2,1)S(1)} %get-tuple-element.33), channel_id=1, source_target_pairs={{0,4},{1,5},{2,6},{3,7},{4,0},{5,1},{6,2},{7,3},{8,12},{9,13},{10,... | collective-permute-start | bytes 589832 | tf_op jit(solution)/shard_map/ppermute | solution.py:386
  111.4 93.7 %collective-permute-start.34 = (bf16[768,128]{1,0:T(8,128)(2,1)S(1)}, bf16[768,128]{1,0:T(8,128)(2,1)S(1)}, u32[]{:S(2)}, u32[]{:S(2)}) collective-permute-start(bf16[768,128]{1,0:T(8,128)(2,1)S(1)} %get-tuple-element.33), channel_id=1, source_target_pairs={{0,2},{1,3},{2,0},{3,1},{4,6},{5,7},{6,4},{7,5},{8,10},{9,11},{10,... | collective-permute-start | bytes 589832 | tf_op jit(solution)/shard_map/ppermute | solution.py:386
  111.5 97.5 %collective-permute-start.26 = (bf16[768,128]{1,0:T(8,128)(2,1)S(1)}, bf16[768,128]{1,0:T(8,128)(2,1)S(1)}, u32[]{:S(2)}, u32[]{:S(2)}) collective-permute-start(bf16[768,128]{1,0:T(8,128)(2,1)S(1)} %get-tuple-element.30), channel_id=1, source_target_pairs={{0,6},{1,7},{2,4},{3,5},{4,2},{5,3},{6,0},{7,1},{8,14},{9,15},{10,... | collective-permute-start | bytes 589832 | tf_op jit(solution)/shard_map/ppermute | solution.py:386
  209.0 75.7 %collective-permute-start.13 = (bf16[3072,128]{1,0:T(8,128)(2,1)S(1)}, bf16[3072,128]{1,0:T(8,128)(2,1)S(1)}, u32[]{:S(2)}, u32[]{:S(2)}) collective-permute-start(bf16[3072,128]{1,0:T(8,128)(2,1)S(1)} %constant_dynamic-update-slice_fusion.refs_0_), channel_id=1, source_target_pairs={{0,8},{1,9},{2,10},{3,11},{4,12},{5,13},{6,14},{7,15},{8,0},{9,1},... | collective-permute-start | bytes 2359304 | tf_op jit(solution)/shard_map/ppermute | solution.py:386
  211.5 30.0 %collective-permute-start.82 = (bf16[768,128]{1,0:T(8,128)(2,1)S(1)}, bf16[768,128]{1,0:T(8,128)(2,1)S(1)}, u32[]{:S(2)}, u32[]{:S(2)}) collective-permute-start(bf16[768,128]{1,0:T(8,128)(2,1)S(1)} %get-tuple-element.45), channel_id=1, source_target_pairs={{0,4},{1,5},{2,6},{3,7},{4,0},{5,1},{6,2},{7,3},{8,12},{9,13},{10,... | collective-permute-start | bytes 589832 | tf_op jit(solution)/shard_map/ppermute | solution.py:386
  284.6 30.7 %collective-permute-start.28 = (bf16[3072,128]{1,0:T(8,128)(2,1)S(1)}, bf16[3072,128]{1,0:T(8,128)(2,1)S(1)}, u32[]{:S(2)}, u32[]{:S(2)}) collective-permute-start(bf16[3072,128]{1,0:T(8,128)(2,1)S(1)} %constant_dynamic-update-slice_fusion.4.refs_8_), channel_id=1, source_target_pairs={{0,1},{1,0},{2,3},{3,2},{4,5},{5,4},{6,7},{7,6},{8,24},{9,25},{10,... | collective-permute-start | bytes 2359304 | tf_op jit(solution)/shard_map/ppermute | solution.py:386
  284.6 34.9 %collective-permute-start.27 = (bf16[3072,128]{1,0:T(8,128)(2,1)S(1)}, bf16[3072,128]{1,0:T(8,128)(2,1)S(1)}, u32[]{:S(2)}, u32[]{:S(2)}) collective-permute-start(bf16[3072,128]{1,0:T(8,128)(2,1)S(1)} %constant_dynamic-update-slice_fusion.4.refs_8_), channel_id=1, source_target_pairs={{0,16},{1,17},{2,18},{3,19},{4,20},{5,21},{6,22},{7,23},{8,9},{9,8... | collective-permute-start | bytes 2359304 | tf_op jit(solution)/shard_map/ppermute | solution.py:386
  302.7 29.5 %collective-permute-start.38 = (bf16[3072,128]{1,0:T(8,128)(2,1)S(1)}, bf16[3072,128]{1,0:T(8,128)(2,1)S(1)}, u32[]{:S(2)}, u32[]{:S(2)}) collective-permute-start(bf16[3072,128]{1,0:T(8,128)(2,1)S(1)} %constant_dynamic-update-slice_fusion.8.refs_16_), channel_id=1, source_target_pairs={{0,1},{1,0},{2,3},{3,2},{4,5},{5,4},{6,7},{7,6},{8,24},{9,25},{10,... | collective-permute-start | bytes 2359304 | tf_op jit(solution)/shard_map/ppermute | solution.py:386
  302.8 33.7 %collective-permute-start.37 = (bf16[3072,128]{1,0:T(8,128)(2,1)S(1)}, bf16[3072,128]{1,0:T(8,128)(2,1)S(1)}, u32[]{:S(2)}, u32[]{:S(2)}) collective-permute-start(bf16[3072,128]{1,0:T(8,128)(2,1)S(1)} %constant_dynamic-update-slice_fusion.8.refs_16_), channel_id=1, source_target_pairs={{0,16},{1,17},{2,18},{3,19},{4,20},{5,21},{6,22},{7,23},{8,9},{9,8... | collective-permute-start | bytes 2359304 | tf_op jit(solution)/shard_map/ppermute | solution.py:386
  319.9 33.4 %collective-permute-start.54 = (bf16[3072,128]{1,0:T(8,128)(2,1)S(1)}, bf16[3072,128]{1,0:T(8,128)(2,1)S(1)}, u32[]{:S(2)}, u32[]{:S(2)}) collective-permute-start(bf16[3072,128]{1,0:T(8,128)(2,1)S(1)} %constant_dynamic-update-slice_fusion.12.refs_24_), channel_id=1, source_target_pairs={{0,16},{1,17},{2,18},{3,19},{4,20},{5,21},{6,22},{7,23},{8,9},{9,8... | collective-permute-start | bytes 2359304 | tf_op jit(solution)/shard_map/ppermute | solution.py:386
  336.4 29.5 %collective-permute-start.65 = (bf16[3072,128]{1,0:T(8,128)(2,1)S(1)}, bf16[3072,128]{1,0:T(8,128)(2,1)S(1)}, u32[]{:S(2)}, u32[]{:S(2)}) collective-permute-start(bf16[3072,128]{1,0:T(8,128)(2,1)S(1)} %constant_dynamic-update-slice_fusion.16.refs_32_), channel_id=1, source_target_pairs={{0,1},{1,0},{2,3},{3,2},{4,5},{5,4},{6,7},{7,6},{8,24},{9,25},{10,... | collective-permute-start | bytes 2359304 | tf_op jit(solution)/shard_map/ppermute | solution.py:386
  336.5 33.7 %collective-permute-start.64 = (bf16[3072,128]{1,0:T(8,128)(2,1)S(1)}, bf16[3072,128]{1,0:T(8,128)(2,1)S(1)}, u32[]{:S(2)}, u32[]{:S(2)}) collective-permute-start(bf16[3072,128]{1,0:T(8,128)(2,1)S(1)} %constant_dynamic-update-slice_fusion.16.refs_32_), channel_id=1, source_target_pairs={{0,16},{1,17},{2,18},{3,19},{4,20},{5,21},{6,22},{7,23},{8,9},{9,8... | collective-permute-start | bytes 2359304 | tf_op jit(solution)/shard_map/ppermute | solution.py:386
  353.3 29.5 %collective-permute-start.75 = (bf16[3072,128]{1,0:T(8,128)(2,1)S(1)}, bf16[3072,128]{1,0:T(8,128)(2,1)S(1)}, u32[]{:S(2)}, u32[]{:S(2)}) collective-permute-start(bf16[3072,128]{1,0:T(8,128)(2,1)S(1)} %constant_dynamic-update-slice_fusion.20.refs_40_), channel_id=1, source_target_pairs={{0,1},{1,0},{2,3},{3,2},{4,5},{5,4},{6,7},{7,6},{8,24},{9,25},{10,... | collective-permute-start | bytes 2359304 | tf_op jit(solution)/shard_map/ppermute | solution.py:386
  353.3 33.7 %collective-permute-start.74 = (bf16[3072,128]{1,0:T(8,128)(2,1)S(1)}, bf16[3072,128]{1,0:T(8,128)(2,1)S(1)}, u32[]{:S(2)}, u32[]{:S(2)}) collective-permute-start(bf16[3072,128]{1,0:T(8,128)(2,1)S(1)} %constant_dynamic-update-slice_fusion.20.refs_40_), channel_id=1, source_target_pairs={{0,16},{1,17},{2,18},{3,19},{4,20},{5,21},{6,22},{7,23},{8,9},{9,8... | collective-permute-start | bytes 2359304 | tf_op jit(solution)/shard_map/ppermute | solution.py:386
  370.1 29.5 %collective-permute-start.85 = (bf16[3072,128]{1,0:T(8,128)(2,1)S(1)}, bf16[3072,128]{1,0:T(8,128)(2,1)S(1)}, u32[]{:S(2)}, u32[]{:S(2)}) collective-permute-start(bf16[3072,128]{1,0:T(8,128)(2,1)S(1)} %constant_dynamic-update-slice_fusion.24.refs_48_), channel_id=1, source_target_pairs={{0,1},{1,0},{2,3},{3,2},{4,5},{5,4},{6,7},{7,6},{8,24},{9,25},{10,... | collective-permute-start | bytes 2359304 | tf_op jit(solution)/shard_map/ppermute | solution.py:386
  370.2 33.7 %collective-permute-start.84 = (bf16[3072,128]{1,0:T(8,128)(2,1)S(1)}, bf16[3072,128]{1,0:T(8,128)(2,1)S(1)}, u32[]{:S(2)}, u32[]{:S(2)}) collective-permute-start(bf16[3072,128]{1,0:T(8,128)(2,1)S(1)} %constant_dynamic-update-slice_fusion.24.refs_48_), channel_id=1, source_target_pairs={{0,16},{1,17},{2,18},{3,19},{4,20},{5,21},{6,22},{7,23},{8,9},{9,8... | collective-permute-start | bytes 2359304 | tf_op jit(solution)/shard_map/ppermute | solution.py:386
  387.0 31.6 %collective-permute-start.94 = (bf16[3072,128]{1,0:T(8,128)(2,1)S(1)}, bf16[3072,128]{1,0:T(8,128)(2,1)S(1)}, u32[]{:S(2)}, u32[]{:S(2)}) collective-permute-start(bf16[3072,128]{1,0:T(8,128)(2,1)S(1)} %constant_dynamic-update-slice_fusion.28.refs_56_), channel_id=1, source_target_pairs={{0,16},{1,17},{2,18},{3,19},{4,20},{5,21},{6,22},{7,23},{8,9},{9,8... | collective-permute-start | bytes 2359304 | tf_op jit(solution)/shard_map/ppermute | solution.py:386
  (133 other events, 4961.8 us)
